TPU v7x, 32 devices: a whole 2x2x4 slice. The times are simulated.
32 devices in a mesh: section: 4 (over x, core), expert: 8 (over z, y).
Axes of the slice: x: 2, y: 2, z: 4, core: 2. Of those that a mesh axis runs over, the one named last changes fastest.
Arguments:
- tokens: bfloat16 [4, 512, 4096], P('section', 'expert'), may hold values from -6 to 6
- out_grad: bfloat16 [4, 512, 4096], P('section', 'expert'), may hold values from -6 to 6
- expert_ids: int32 [4, 512, 2], P('section', 'expert'), may hold values from 0 to 7, as said below
- slot_ids: int32 [4, 512, 2], P('section', 'expert'), may hold values from 0 to 15, as said below
- gate_int: int32 [4, 512, 2], P('section', 'expert'), may hold values from 16 to 255
- saved_gate: bfloat16 [4, 128, 14336], P('section', None, 'expert'), may hold values from -6 to 6
- saved_up: bfloat16 [4, 128, 14336], P('section', None, 'expert'), may hold values from -6 to 6
- w_gate: bfloat16 [4, 4096, 14336], P('section', None, 'expert'), may hold values from -0.09375 to 0.09375
- w_up: bfloat16 [4, 4096, 14336], P('section', None, 'expert'), may hold values from -0.09375 to 0.09375
- w_down: bfloat16 [4, 14336, 4096], P('section', 'expert'), may hold values from -0.0625 to 0.0625
Outputs:
- arriving_grad: bfloat16 [4, 512, 4096], P('section', 'expert')
- grad_w_gate: bfloat16 [4, 4096, 14336], P('section', None, 'expert')
- grad_w_up: bfloat16 [4, 4096, 14336], P('section', None, 'expert')
- grad_w_down: bfloat16 [4, 14336, 4096], P('section', 'expert')
Inputs may be any that keep to these rules, and one draw needn't show every extreme that they name: `expert_ids`: in each section, the 64 tokens of each index of expert name each of the 8 experts exactly 16 times; a token's two experts differ. `slot_ids`: for each expert, the slots of the 64 tokens of one index of expert that name it are 0 to 15, each once.
All inputs are finite; a program needn't handle non-finite values.
Results may differ from a plain program's by a relative error of at most 0.018.
Values may be sent and summed in bfloat16 or wider, within the bound.
No kernel may reach another device: no remote copies, remote signals or barrier semaphores. Data moves between devices by JAX's collectives and lax.ppermute only.
A program may use at most 128 MiB of HBM per device.

v0:
```python
import jax
import jax.numpy as jnp
from jax import lax
from jax.sharding import PartitionSpec as P

EXPERTS = 8
E_WIN = 2


def from_behind(x, axis, by):
    peers = lax.axis_size(axis)
    pairs = [(i, i + by) for i in range(peers) if 0 <= i + by < peers]
    return lax.ppermute(x, axis, pairs)


def shards(
    tokens, out_grad, expert_ids, slot_ids, gate_int, saved_gate, saved_up, w_gate, w_up, w_down
):
    inputs = tokens[0]
    upstream_grad = out_grad[0]
    chosen = expert_ids[0]
    places = slot_ids[0]
    weights_k = gate_int[0].astype(jnp.float32) / 256.0
    devices = lax.axis_size("expert")
    per_expert = devices // E_WIN
    capacity = inputs.shape[0] * 2 // EXPERTS
    slot_count = E_WIN * capacity
    model_width = inputs.shape[1]
    target = chosen * capacity + places
    columns = lax.broadcasted_iota(jnp.int32, (1, 1, slot_count), 2)
    placed = jnp.logical_and(target[:, :, None] == columns, chosen[:, :, None] < E_WIN).astype(
        jnp.float32
    )
    selector = jnp.sum(placed, axis=1)
    scaled = jnp.sum(placed * weights_k[:, :, None], axis=1)
    send_inputs = jnp.einsum(
        "tc,td->cd", selector.astype(jnp.bfloat16), inputs, preferred_element_type=jnp.float32
    ).astype(jnp.bfloat16)
    send_grads = jnp.einsum(
        "tc,td->cd", scaled.astype(jnp.bfloat16), upstream_grad, preferred_element_type=jnp.float32
    ).astype(jnp.bfloat16)
    send_inputs = jnp.repeat(send_inputs.reshape(E_WIN, capacity, model_width), per_expert, axis=0)
    send_grads = jnp.repeat(send_grads.reshape(E_WIN, capacity, model_width), per_expert, axis=0)
    recv_inputs, recv_grads = (
        lax.all_to_all(send_inputs, "expert", split_axis=0, concat_axis=0, tiled=True),
        lax.all_to_all(send_grads, "expert", split_axis=0, concat_axis=0, tiled=True),
    )
    rows_in = recv_inputs.reshape(-1, model_width)
    rows_grad = recv_grads.reshape(-1, model_width)
    gate_pre = saved_gate[0].astype(jnp.float32)
    up_pre = saved_up[0].astype(jnp.float32)
    sigmoid_g = jax.nn.sigmoid(gate_pre)
    activated = gate_pre * sigmoid_g
    hidden = (activated * up_pre).astype(jnp.bfloat16)
    hidden_grad = jnp.einsum("rd,hd->rh", rows_grad, w_down[0], preferred_element_type=jnp.float32)
    gate_grad = (hidden_grad * up_pre * sigmoid_g * (1.0 + gate_pre * (1.0 - sigmoid_g))).astype(
        jnp.bfloat16
    )
    up_grad = (hidden_grad * activated).astype(jnp.bfloat16)
    partial_rows = jnp.einsum("rh,dh->rd", gate_grad, w_gate[0], preferred_element_type=jnp.float32)
    partial_rows = (
        partial_rows + jnp.einsum("rh,dh->rd", up_grad, w_up[0], preferred_element_type=jnp.float32)
    ).astype(jnp.bfloat16)
    grad_down = jnp.einsum(
        "rh,rd->hd", hidden, rows_grad, preferred_element_type=jnp.float32
    ).astype(jnp.bfloat16)
    grad_gate = jnp.einsum(
        "rd,rh->dh", rows_in, gate_grad, preferred_element_type=jnp.float32
    ).astype(jnp.bfloat16)
    grad_up = jnp.einsum("rd,rh->dh", rows_in, up_grad, preferred_element_type=jnp.float32).astype(
        jnp.bfloat16
    )
    returned = lax.all_to_all(
        partial_rows.reshape(devices, capacity, model_width),
        "expert",
        split_axis=0,
        concat_axis=0,
        tiled=True,
    )
    summed = jnp.sum(
        returned.astype(jnp.float32).reshape(E_WIN, per_expert, capacity, model_width), axis=1
    )
    combined = jnp.einsum(
        "tc,cd->td",
        selector,
        summed.reshape(slot_count, model_width),
        precision=lax.Precision.HIGHEST,
    ).astype(jnp.bfloat16)
    arriving = from_behind(combined, "section", -1)
    return (arriving[None], grad_gate[None], grad_up[None], grad_down[None])


def solution(mesh):
    return jax.shard_map(
        shards,
        mesh=mesh,
        in_specs=(
            P("section", "expert", None),
            P("section", "expert", None),
            P("section", "expert", None),
            P("section", "expert", None),
            P("section", "expert", None),
            P("section", None, "expert"),
            P("section", None, "expert"),
            P("section", None, "expert"),
            P("section", None, "expert"),
            P("section", "expert", None),
        ),
        out_specs=(
            P("section", "expert", None),
            P("section", None, "expert"),
            P("section", None, "expert"),
            P("section", "expert", None),
        ),
        check_vma=False,
    )
```

profile of v0, /device:TPU:0, one launch (start us, length us, event | category | flops | bytes accessed | tf_op | source)
XLA Modules:
  0.0 144.7 jit_solution(7941068290067626400)
XLA Ops:
  0.6 0.0 copy-start
  0.6 0.0 copy-start.2
  0.7 0.8 compare_bitcast_fusion
  1.4 0.7 add_bitcast_fusion
  2.1 0.7 multiply_bitcast_fusion
  2.8 0.0 copy-done
  2.8 0.2 convolution_convert_fusion.5
  3.1 0.1 broadcast_in_dim.20
  3.2 32.9 %all_to_all.15 = bf16[8,16,4096]{2,1,0:T(8,128)(2,1)S(1)} all-to-all(bf16[8,16,4096]{2,1,0:T(8,128)(2,1)S(1)} %bitcast.100), channel_id=1, replica_groups=mesh['section'=4,'expert'=8] {'expert'}, dimensions={0} | all-to-all | bytes 2097152 | tf_op jit(solution)/shard_map/all_to_all | solution.py:46
  36.0 10.4 %fusion.21 = (bf16[128,1792]{1,0:T(8,128)(2,1)S(1)}, f32[128,1792]{1,0:T(8,128)S(1)}) fusion(bf16[1,128,1792]{2,1,0:T(8,128)(2,1)} %param.16, bf16[1,128,1792]{2,1,0:T(8,128)(2,1)} %param.15, bf16[128,4096]{1,0:T(8,128)(2,1)S(1)} %bitcast.97, bf16[1,1792,4096]{2,1,0:T(8,128)(2,1)} %param.19), kind=kOutput, calls=%fused_computation.29 | convolution fusion | flops 1881800704 | bytes 18022400 | tf_op jit(solution)/shard_map/rd,hd->rh/dot_general | solution.py:55
  46.4 0.0 copy-start.5
  46.4 0.0 copy-done.2
  46.4 10.3 %fusion = f32[128,4096]{1,0:T(8,128)S(1)} fusion(bf16[1,4096,1792]{2,1,0:T(8,128)(2,1)} %param.18, f32[128,1792]{1,0:T(8,128)S(1)} %get-tuple-element.7, bf16[1,128,1792]{2,1,0:T(8,128)(2,1)S(1)} %copy-done.2), kind=kOutput, calls=%fused_computation.3 | convolution fusion | flops 1880653824 | bytes 18153472 | tf_op jit(solution)/shard_map/rh,dh->rd/dot_general | solution.py:62
  56.7 10.9 %fusion.12 = bf16[128,4096]{1,0:T(8,128)(2,1)} fusion(f32[128,4096]{1,0:T(8,128)S(1)} %fusion, bf16[128,1792]{1,0:T(8,128)(2,1)S(1)} %get-tuple-element.6, bf16[1,4096,1792]{2,1,0:T(8,128)(2,1)} %param.17), kind=kOutput, calls=%fused_computation.13 | convolution fusion | flops 1880096768 | bytes 18284544 | tf_op jit(solution)/shard_map/rh,dh->rd/dot_general | solution.py:60
  67.7 0.0 copy-done.5
  67.7 3.6 %all-to-all-start.1 = ((bf16[8,16,4096]{2,1,0:T(8,128)(2,1)}), bf16[8,16,4096]{2,1,0:T(8,128)(2,1)S(1)}, u32[]{:S(2)}, u32[]{:S(2)}) async-start(bf16[8,16,4096]{2,1,0:T(8,128)(2,1)} %bitcast.12), calls=%async_computation.1 | async-start | bytes 2097152 | tf_op jit(solution)/shard_map/all_to_all | solution.py:73
  71.3 1.2 convolution_convert_fusion.4
  72.5 24.3 %all-to-all-done.1 = bf16[8,16,4096]{2,1,0:T(8,128)(2,1)S(1)} async-done(((bf16[8,16,4096]{2,1,0:T(8,128)(2,1)}), bf16[8,16,4096]{2,1,0:T(8,128)(2,1)S(1)}, u32[]{:S(2)}, u32[]{:S(2)}) %all-to-all-start.1) | async-done | bytes 1048608 | tf_op jit(solution)/shard_map/all_to_all | solution.py:73
  96.8 0.0 copy-start.3
  96.8 1.2 broadcast_in_dim.22
  98.0 0.1 copy-done.3
  98.2 3.7 %all-to-all-start.2 = ((bf16[8,16,4096]{2,1,0:T(8,128)(2,1)}), bf16[8,16,4096]{2,1,0:T(8,128)(2,1)S(1)}, u32[]{:S(2)}, u32[]{:S(2)}) async-start(bf16[8,16,4096]{2,1,0:T(8,128)(2,1)} %bitcast.99), calls=%async_computation.2 | async-start | bytes 2097152 | tf_op jit(solution)/shard_map/all_to_all | solution.py:45
  101.9 0.0 copy-start.4
  101.9 8.7 %fusion.8 = bf16[1,1792,4096]{2,1,0:T(8,128)(2,1)} fusion(bf16[128,4096]{1,0:T(8,128)(2,1)S(1)} %bitcast.98, bf16[1,128,1792]{2,1,0:T(8,128)(2,1)} %param.16, bf16[1,128,1792]{2,1,0:T(8,128)(2,1)S(1)} %copy-done.2), kind=kOutput, calls=%fused_computation.11 | convolution fusion | flops 1888223232 | bytes 16646144 | tf_op jit(solution)/shard_map/rh,rd->hd/dot_general | solution.py:64
  110.6 0.0 copy-done.4
  110.6 0.0 copy-start.6
  110.6 0.2 convert_reduce_fusion
  110.8 1.8 %convolution_convert_fusion.3 = bf16[64,4096]{1,0:T(8,128)(2,1)} fusion(f32[64,32]{0,1:T(8,128)S(1)} %get-tuple-element.5, f32[32,4096]{1,0:T(8,128)S(1)} %bitcast.101), kind=kOutput, calls=%fused_computation.14 | convolution fusion | flops 100925440 | bytes 1056768 | tf_op jit(solution)/shard_map/tc,cd->td/dot_general | solution.py:83
  112.6 1.3 collective-permute-start
  113.9 13.7 %all-to-all-done.2 = bf16[8,16,4096]{2,1,0:T(8,128)(2,1)S(1)} async-done(((bf16[8,16,4096]{2,1,0:T(8,128)(2,1)}), bf16[8,16,4096]{2,1,0:T(8,128)(2,1)S(1)}, u32[]{:S(2)}, u32[]{:S(2)}) %all-to-all-start.2) | async-done | bytes 1048608 | tf_op jit(solution)/shard_map/all_to_all | solution.py:45
  127.6 0.0 copy-start.1
  127.6 7.6 %fusion.6 = bf16[1,4096,1792]{2,1,0:T(8,128)(2,1)} fusion(bf16[128,4096]{1,0:T(8,128)(2,1)S(1)} %bitcast.95, bf16[128,1792]{1,0:T(8,128)(2,1)S(1)} %get-tuple-element.6), kind=kOutput, calls=%fused_computation.9 | convolution fusion | flops 1886388224 | bytes 16187392 | tf_op jit(solution)/shard_map/rd,rh->dh/dot_general | solution.py:67
  135.2 0.0 copy-done.6
  135.2 7.6 %fusion.7 = bf16[1,4096,1792]{2,1,0:T(8,128)(2,1)} fusion(bf16[128,4096]{1,0:T(8,128)(2,1)S(1)} %bitcast.96, f32[128,1792]{1,0:T(8,128)S(1)} %copy-done.6, bf16[1,128,1792]{2,1,0:T(8,128)(2,1)S(1)} %copy-done.2), kind=kOutput, calls=%fused_computation.10 | convolution fusion | flops 1887993856 | bytes 17104896 | tf_op jit(solution)/shard_map/rd,rh->dh/dot_general | solution.py:70
  142.8 0.0 collective-permute-done
  142.8 1.9 %copy.18 = bf16[1,64,4096]{2,1,0:T(8,128)(2,1)} copy(bf16[1,64,4096]{2,1,0:T(8,128)(2,1)} %bitcast.15) | data formatting | bytes 1048576
  144.7 0.0 copy-done.1
  (1 shorter events, 0.0 us)
Async XLA Ops:
  0.6 2.2 %copy-start = (bf16[1,64,4096]{2,1,0:T(8,128)(2,1)S(1)}, bf16[1,64,4096]{2,1,0:T(8,128)(2,1)}, u32[]{:S(2)}) copy-start(bf16[1,64,4096]{2,1,0:T(8,128)(2,1)} %param.11) | copy-start | bytes 1572868
  0.6 45.8 %copy-start.2 = (bf16[1,128,1792]{2,1,0:T(8,128)(2,1)S(1)}, bf16[1,128,1792]{2,1,0:T(8,128)(2,1)}, u32[]{:S(2)}) copy-start(bf16[1,128,1792]{2,1,0:T(8,128)(2,1)} %param.15) | copy-start | bytes 1376260
  46.4 21.3 %copy-start.5 = (f32[128,1792]{1,0:T(8,128)}, f32[128,1792]{1,0:T(8,128)S(1)}, u32[]{:S(2)}) copy-start(f32[128,1792]{1,0:T(8,128)S(1)} %get-tuple-element.7) | copy-start | bytes 2752516
  67.7 29.2 %all-to-all-start.1 = ((bf16[8,16,4096]{2,1,0:T(8,128)(2,1)}), bf16[8,16,4096]{2,1,0:T(8,128)(2,1)S(1)}, u32[]{:S(2)}, u32[]{:S(2)}) async-start(bf16[8,16,4096]{2,1,0:T(8,128)(2,1)} %bitcast.12), calls=%async_computation.1 | async-start | bytes 2097152 | tf_op jit(solution)/shard_map/all_to_all | solution.py:73
  96.8 1.3 copy-start.3
  98.2 29.5 %all-to-all-start.2 = ((bf16[8,16,4096]{2,1,0:T(8,128)(2,1)}), bf16[8,16,4096]{2,1,0:T(8,128)(2,1)S(1)}, u32[]{:S(2)}, u32[]{:S(2)}) async-start(bf16[8,16,4096]{2,1,0:T(8,128)(2,1)} %bitcast.99), calls=%async_computation.2 | async-start | bytes 2097152 | tf_op jit(solution)/shard_map/all_to_all | solution.py:45
  101.9 8.7 %copy-start.4 = (bf16[8,16,4096]{2,1,0:T(8,128)(2,1)S(1)}, bf16[8,16,4096]{2,1,0:T(8,128)(2,1)}, u32[]{:S(2)}) copy-start(bf16[8,16,4096]{2,1,0:T(8,128)(2,1)} %copy-done.3) | copy-start | bytes 3145732
  110.6 24.6 %copy-start.6 = (f32[128,1792]{1,0:T(8,128)S(1)}, f32[128,1792]{1,0:T(8,128)}, u32[]{:S(2)}) copy-start(f32[128,1792]{1,0:T(8,128)} %copy-done.5) | copy-start | bytes 2752516
  112.6 30.2 %collective-permute-start = (bf16[64,4096]{1,0:T(8,128)(2,1)}, bf16[64,4096]{1,0:T(8,128)(2,1)}, u32[]{:S(2)}, u32[]{:S(2)}) collective-permute-start(bf16[64,4096]{1,0:T(8,128)(2,1)} %convolution_convert_fusion.3), channel_id=1, source_target_pairs={{8,0},{16,8},{24,16},{9,1},{17,9},{25,17},{10,2},{18,10},{26,18},{... | collective-permute-start | bytes 1572872 | tf_op jit(solution)/shard_map/ppermute | solution.py:13
  127.6 17.0 %copy-start.1 = (bf16[1,64,4096]{2,1,0:T(8,128)(2,1)S(1)}, bf16[1,64,4096]{2,1,0:T(8,128)(2,1)}, u32[]{:S(2)}) copy-start(bf16[1,64,4096]{2,1,0:T(8,128)(2,1)} %param.11) | copy-start | bytes 1572868
where the time goes:
time: 145 us
  matrix products  58.7 us (40%)
  waiting for transfers between devices  38 us (26%)
  blocking collectives  32.9 us (23%)
  starting transfers between devices  8.62 us (6%)
  local copies, waits for them, and re-layouts  3.31 us (2%)
  other arithmetic  2.33 us (2%)
    all_to_all x1, blocking collectives, shards(): lax.all_to_all(send_grads, 'expert', split_axis=0, concat_axis=0, tiled=T...  32.9 us
    all_to_all x1, waiting for transfers between devices, shards(): lax.all_to_all(partial_rows.reshape(devices, capacity, model_width), 'exp...  24.3 us
    all_to_all x1, waiting for transfers between devices, shards(): lax.all_to_all(send_inputs, 'expert', split_axis=0, concat_axis=0, tiled=...  13.7 us
    dot_general x1, matrix products, shards(): jnp.einsum('rh,dh->rd', gate_grad, w_gate[0], preferred_element_type=jnp....  10.9 us
    dot_general x1, matrix products, shards(): jnp.einsum('rd,hd->rh', rows_grad, w_down[0], preferred_element_type=jnp....  10.4 us
    dot_general x1, matrix products, shards(): jnp.einsum('rh,dh->rd', up_grad, w_up[0], preferred_element_type=jnp.floa...  10.3 us
    dot_general x1, matrix products, shards(): jnp.einsum('rh,rd->hd', hidden, rows_grad, preferred_element_type=jnp.flo...  8.71 us
    dot_general x1, matrix products, shards(): jnp.einsum('rd,rh->dh', rows_in, up_grad, preferred_element_type=jnp.floa...  7.58 us
  transfers between devices with their start and end apart: 3, of which 2 were waited for; matrix products, arithmetic and copies ran while one was open for 19% of the time, Pallas kernels for 0%

commit v1 on v0

v1 whole, which is shorter than its diff:
```python
import functools

import jax
import jax.numpy as jnp
from jax import lax
from jax.experimental import pallas as pl
from jax.experimental.pallas import tpu as pltpu
from jax.sharding import PartitionSpec as P


EXPERTS = 8
E_WIN = 2
BF16 = jnp.bfloat16
F32 = jnp.float32
NT = (((1,), (1,)), ((), ()))
TN = (((0,), (0,)), ((), ()))
NN = (((1,), (0,)), ((), ()))
MIB = 2**20


def vmem():
    return pl.BlockSpec(memory_space=pltpu.VMEM)


def anywhere():
    return pl.BlockSpec(memory_space=pl.ANY)


def hbm():
    return pl.BlockSpec(memory_space=pltpu.HBM)


def smem():
    return pl.BlockSpec(memory_space=pltpu.SMEM)


def piece(total, wanted):
    for size in (wanted, 512, 256, 128):
        if size <= wanted and total % size == 0:
            return size
    return total


def like(shape, dtype=BF16):
    return jax.ShapeDtypeStruct(shape, dtype)


def params(mib):
    return pltpu.CompilerParams(vmem_limit_bytes=int(mib * MIB))


def placement(half, ids, slots, weights, capacity):
    rows = lax.broadcasted_iota(jnp.int32, (2 * capacity, ids.shape[1]), 0)
    matrix = jnp.zeros(rows.shape, F32)
    for k in range(2):
        expert = ids[k : k + 1, :]
        place = jnp.where(expert == half, 0, capacity) + slots[k : k + 1, :]
        hit = jnp.logical_and(rows == place, expert < E_WIN)
        matrix += jnp.where(hit, weights[k : k + 1, :], 0.0)
    return matrix.astype(BF16)


def pick_kernel(capacity, half_ref, *refs):
    sources, outs, copies, sems = refs[:5], refs[5:10], refs[10:15], refs[15]
    half = half_ref[0]
    flying = [
        pltpu.make_async_copy(source, copy, sems.at[n])
        for n, (source, copy) in enumerate(zip(sources, copies))
    ]
    for copy in flying:
        copy.start()
    for copy in flying[:4]:
        copy.wait()
    ids, slots, gates = (copies[n][...] for n in range(3))
    grads_own, grads_far, in_own, in_far, tables = outs
    scaled = placement(half, ids, slots, gates.astype(F32) / 256.0, capacity)
    plain = placement(half, ids, slots, jnp.ones(ids.shape, F32), capacity)
    rows = lax.dot_general(scaled, copies[3][...], NN, preferred_element_type=F32).astype(BF16)
    grads_own[...] = rows[:capacity]
    grads_far[...] = rows[capacity:]
    tables[:2, :] = ids
    tables[2:, :] = slots
    flying[4].wait()
    rows = lax.dot_general(plain, copies[4][...], NN, preferred_element_type=F32).astype(BF16)
    in_own[...] = rows[:capacity]
    in_far[...] = rows[capacity:]


def pick(half, ids, slots, gates, grads, tokens, capacity):
    width = tokens.shape[1]
    sources = (ids, slots, gates, grads, tokens)
    return pl.pallas_call(
        functools.partial(pick_kernel, capacity),
        in_specs=[smem()] + [hbm()] * len(sources),
        out_specs=[vmem()] * 5,
        out_shape=[like((capacity, width))] * 4 + [like((4, ids.shape[1]), jnp.int32)],
        scratch_shapes=[pltpu.VMEM(x.shape, x.dtype) for x in sources]
        + [pltpu.SemaphoreType.DMA((len(sources),))],
        compiler_params=params(8),
        cost_estimate=pl.CostEstimate(
            flops=2**36, bytes_accessed=6 * tokens.size, transcendentals=0
        ),
    )(half, *sources)


def hidden_kernel(capacity, pairs, index_ref, *refs):
    blocks = refs[: len(pairs)]
    gate_hbm, up_hbm, w_down, rows, gate_grad, up_grad, hidden = refs[len(pairs) : len(pairs) + 7]
    gate, up, block_sems, saved_sems = refs[len(pairs) + 7 :]
    landings = land(capacity, pairs, index_ref[0], blocks, rows, block_sems)
    saved = [
        pltpu.make_async_copy(gate_hbm, gate, saved_sems.at[0]),
        pltpu.make_async_copy(up_hbm, up, saved_sems.at[1]),
    ]
    for copy in landings + saved:
        copy.start()
    for copy in landings + saved:
        copy.wait()
    units, step = w_down.shape[0], 256
    for start in range(0, units, step):
        some = slice(start, min(start + step, units))
        grad = lax.dot_general(rows[...], w_down[some, :], NT, preferred_element_type=F32)
        g = gate[:, some].astype(F32)
        u = up[:, some].astype(F32)
        s = jax.nn.sigmoid(g)
        act = g * s
        hidden[:, some] = (act * u).astype(BF16)
        gate_grad[:, some] = (grad * u * s * (1.0 + g * (1.0 - s))).astype(BF16)
        up_grad[:, some] = (grad * act).astype(BF16)


def hidden_stage(index, blocks, pairs, gate, up, w_down, capacity):
    units, width = w_down.shape
    total = gate.shape[0]
    return pl.pallas_call(
        functools.partial(hidden_kernel, capacity, pairs),
        in_specs=[smem()] + [anywhere()] * len(blocks) + [hbm()] * 2 + [vmem()],
        out_specs=[vmem()] * 4,
        out_shape=[like((total, width))] + [like((total, units))] * 3,
        scratch_shapes=[
            pltpu.VMEM((total, units), BF16),
            pltpu.VMEM((total, units), BF16),
            pltpu.SemaphoreType.DMA((total // capacity,)),
            pltpu.SemaphoreType.DMA((2,)),
        ],
        compiler_params=params(6),
        cost_estimate=pl.CostEstimate(
            flops=2 * total * units * width, bytes_accessed=2 * units * width, transcendentals=0
        ),
    )(index, *blocks, gate, up, w_down)


def part_kernel(capacity, group, step, index_ref, *refs):
    gate_grad, up_grad, w_gate, w_up = refs[:4]
    outs, stage = refs[4 : 4 + group], refs[4 + group]
    index = index_ref[0]
    for i in range(w_gate.shape[0] // step):
        some = slice(i * step, (i + 1) * step)
        part = lax.dot_general(gate_grad[...], w_gate[some, :], NT, preferred_element_type=F32)
        part += lax.dot_general(up_grad[...], w_up[some, :], NT, preferred_element_type=F32)
        stage[i % 2] = part.astype(BF16)
        for m in range(2 * group):
            source = pl.multiple_of(jnp.bitwise_xor(index, m) * capacity, capacity)
            start = m // group * capacity
            outs[m % group][start : start + capacity, some] = stage[
                i % 2, pl.ds(source, capacity), :
            ]


def part_stage(index, gate_grad, up_grad, w_gate, w_up, capacity, group):
    width, units = w_gate.shape
    total = gate_grad.shape[0]
    step = piece(width, 512)
    return pl.pallas_call(
        functools.partial(part_kernel, capacity, group, step),
        in_specs=[smem()] + [vmem()] * 4,
        out_specs=[vmem()] * group,
        out_shape=[like((2 * capacity, width))] * group,
        scratch_shapes=[pltpu.VMEM((2, total, step), BF16)],
        compiler_params=params(6),
        cost_estimate=pl.CostEstimate(
            flops=4 * total * units * width, bytes_accessed=4 * units * width, transcendentals=0
        ),
    )(index, gate_grad, up_grad, w_gate, w_up)


def land(capacity, pairs, index, blocks, rows, sems):
    copies = []
    for block, members in zip(blocks, pairs):
        for part, m in enumerate(members):
            start = pl.multiple_of(jnp.bitwise_xor(index, m) * capacity, capacity)
            copies.append(
                pltpu.make_async_copy(
                    block.at[pl.ds(part * capacity, capacity)],
                    rows.at[pl.ds(start, capacity)],
                    sems.at[m],
                )
            )
    return copies


def weight_body(step, depth, left, right, out, ring, sems):
    flying = [None] * depth
    for i in range(left.shape[1] // step):
        slot = i % depth
        value = lax.dot_general(
            left[:, i * step : (i + 1) * step], right[...], TN, preferred_element_type=F32
        ).astype(BF16)
        if flying[slot] is not None:
            flying[slot].wait()
        ring[slot] = value
        copy = pltpu.make_async_copy(ring.at[slot], out.at[pl.ds(i * step, step)], sems.at[slot])
        copy.start()
        flying[slot] = copy
    for copy in flying:
        if copy is not None:
            copy.wait()


def landing_kernel(capacity, pairs, step, depth, index_ref, *refs):
    blocks = refs[: len(pairs)]
    right, out, rows, ring, sems, block_sems = refs[len(pairs) :]
    copies = land(capacity, pairs, index_ref[0], blocks, rows, block_sems)
    for copy in copies:
        copy.start()
    for copy in copies:
        copy.wait()
    weight_body(step, depth, rows, right, out, ring, sems)


def weight_sizes(rows, columns, total, wanted):
    step = piece(rows, wanted)
    depth = min(4, rows // step)
    return step, depth, dict(
        compiler_params=params(32),
        cost_estimate=pl.CostEstimate(
            flops=2 * total * rows * columns, bytes_accessed=2 * rows * columns, transcendentals=0
        ),
    )


def weight_stage(left, right, wanted):
    total, rows = left.shape
    columns = right.shape[1]
    step, depth, more = weight_sizes(rows, columns, total, wanted)
    return pl.pallas_call(
        functools.partial(weight_body, step, depth),
        in_specs=[vmem()] * 2,
        out_specs=hbm(),
        out_shape=like((rows, columns)),
        scratch_shapes=[
            pltpu.VMEM((depth, step, columns), BF16),
            pltpu.SemaphoreType.DMA((depth,)),
        ],
        **more,
    )(left, right)


def landing_stage(index, blocks, pairs, right, wanted, capacity):
    total, columns = right.shape
    rows = blocks[0].shape[1]
    step, depth, more = weight_sizes(rows, columns, total, wanted)
    return pl.pallas_call(
        functools.partial(landing_kernel, capacity, pairs, step, depth),
        in_specs=[smem()] + [anywhere()] * len(blocks) + [vmem()],
        out_specs=[hbm(), vmem()],
        out_shape=[like((rows, columns)), like((total, rows))],
        scratch_shapes=[
            pltpu.VMEM((depth, step, columns), BF16),
            pltpu.SemaphoreType.DMA((depth,)),
            pltpu.SemaphoreType.DMA((total // capacity,)),
        ],
        **more,
    )(index, *blocks, right)


def join_kernel(capacity, shares, half_ref, tables, *refs):
    out_ref = refs[-1]
    ones = jnp.ones((2, tables.shape[1]), F32)
    matrix = placement(half_ref[0], tables[:2, :], tables[2:, :], ones, capacity)
    width = out_ref.shape[1] // shares
    for share in range(shares):
        own, far = refs[2 * share : 2 * share + 2]
        total = lax.dot_general(matrix[:capacity], own[...], TN, preferred_element_type=F32)
        total += lax.dot_general(matrix[capacity:], far[...], TN, preferred_element_type=F32)
        out_ref[:, share * width : (share + 1) * width] = total.astype(BF16)


def join(half, tables, pieces, capacity):
    shares = len(pieces) // 2
    return pl.pallas_call(
        functools.partial(join_kernel, capacity, shares),
        in_specs=[smem()] + [vmem()] * (1 + len(pieces)),
        out_specs=vmem(),
        out_shape=like((tables.shape[1], shares * pieces[0].shape[1])),
        compiler_params=params(8),
    )(half, tables, *pieces)


def to_partner(value, m):
    peers = lax.axis_size("expert")
    return lax.ppermute(value, "expert", [(i, i ^ m) for i in range(peers)])


def to_behind(value, m):
    peers, layers = lax.axis_size("expert"), lax.axis_size("section")
    pairs = [
        (s * peers + i, (s - 1) * peers + (i ^ m)) for s in range(1, layers) for i in range(peers)
    ]
    return lax.ppermute(value, ("section", "expert"), pairs)


def shards(
    tokens, out_grad, expert_ids, slot_ids, gate_int, saved_gate, saved_up, w_gate, w_up, w_down
):
    peers = lax.axis_size("expert")
    group = peers // E_WIN
    capacity = tokens.shape[1] * 2 // EXPERTS
    stay = functools.partial(pltpu.with_memory_space_constraint, memory_space=pltpu.HBM)
    place = lax.axis_index("expert").astype(jnp.int32)
    index = place.reshape(1)
    half = (place // group).reshape(1)
    shares = 1

    grads_own, grads_far, in_own, in_far, tables = pick(
        half,
        stay(expert_ids[0].T),
        stay(slot_ids[0].T),
        stay(gate_int[0].T),
        stay(out_grad[0]),
        stay(tokens[0]),
        capacity,
    )
    crossed = to_partner(grads_far, group)
    near = [grads_own] + [to_partner(grads_own, m) for m in range(1, group)]
    tables = to_behind(tables, 0)
    far = [crossed] + [to_partner(crossed, m) for m in range(1, group)]
    in_crossed = to_partner(in_far, group)
    singles = [(m,) for m in range(2 * group)]
    rows_grad, gate_grad, up_grad, hidden = hidden_stage(
        index,
        near + far,
        singles,
        stay(saved_gate[0]),
        stay(saved_up[0]),
        w_down[0],
        capacity,
    )
    both = jnp.concatenate([in_own, in_crossed], axis=0)
    in_blocks = [both] + [to_partner(both, m) for m in range(1, group)]
    parts, returned = [], []
    for share in range(shares):
        parts.append(
            part_stage(
                index,
                gate_grad,
                up_grad,
                w_gate[0],
                w_up[0],
                capacity,
                group,
            )
        )
        returned.append([to_partner(parts[share][m], m) for m in range(1, group)])
    grad_down = weight_stage(hidden, rows_grad, 256)
    pieces = []
    for share in range(shares):
        summed = parts[share][0].astype(F32)
        for part in returned[share]:
            summed += part.astype(F32)
        summed = summed.astype(BF16)
        kept, sent = summed[:capacity], summed[capacity:]
        sent = to_behind(sent, group)
        kept = to_behind(kept, 0)
        pieces += [kept, sent]
    pairs = [(m, m + group) for m in range(group)]
    grad_gate, rows_in = landing_stage(index, in_blocks, pairs, gate_grad, 512, capacity)
    grad_up = weight_stage(rows_in, up_grad, 512)
    arriving = join(half, tables, pieces, capacity)
    return (arriving[None], grad_gate[None], grad_up[None], grad_down[None])


def solution(mesh):
    rows = P("section", "expert", None)
    columns = P("section", None, "expert")
    return jax.shard_map(
        shards,
        mesh=mesh,
        in_specs=(rows,) * 5 + (columns,) * 4 + (rows,),
        out_specs=(rows, columns, columns, rows),
        check_vma=False,
    )
```

time: 145 us -> 92.2 us (0.64)
  the two profiles are of different devices: /device:TPU:0 before, /device:TPU:3 now
where the time goes in v1:
time: 92.2 us; the launch traced here: 92 us
  Pallas kernels  42.3 us (46%)
  starting transfers between devices  33.6 us (36%)
  waiting for transfers between devices  9.77 us (11%)
  local copies, waits for them, and re-layouts  5.23 us (6%)
    ppermute x14, starting transfers between devices, to_partner(): return lax.ppermute(value, 'expert', [(i, i ^ m) for i in range(peers)])  21.4 us
    pallas_call x2, Pallas kernels, weight_stage(): pl.pallas_call(functools.partial(weight_body, step, depth), in_specs=[vme...  13.7 us
    ppermute x3, starting transfers between devices, to_behind(): return lax.ppermute(value, ('section', 'expert'), pairs)  12.3 us
    ppermute x14, waiting for transfers between devices, to_partner(): return lax.ppermute(value, 'expert', [(i, i ^ m) for i in range(peers)])  9.76 us
    pallas_call x1, Pallas kernels, part_stage(): pl.pallas_call(functools.partial(part_kernel, capacity, group, step), in_...  9.43 us
    pallas_call x1, Pallas kernels, landing_stage(): pl.pallas_call(functools.partial(landing_kernel, capacity, pairs, step, d...  8.49 us
    pallas_call x1, Pallas kernels, hidden_stage(): pl.pallas_call(functools.partial(hidden_kernel, capacity, pairs), in_spec...  7.69 us
    unnamed x13, local copies, waits for them, and re-layouts  5.2 us
  transfers between devices with their start and end apart: 17, of which 3 were waited for; matrix products, arithmetic and copies ran while one was open for 0% of the time, Pallas kernels for 43%

profile of v1, /device:TPU:3, one launch (start us, length us, event | category | flops | bytes accessed | tf_op | source)
XLA Modules:
  0.0 92.0 jit_solution(7684148364259037976)
XLA Ops:
  0.6 0.0 slice-start
  0.7 0.0 copy-start
  0.7 0.0 slice-start.1
  0.7 0.0 slice-start.2
  0.7 0.0 slice-start.3
  0.7 1.7 %shard_map.129 = (bf16[16,4096]{1,0:T(8,128)(2,1)S(1)}, bf16[16,4096]{1,0:T(8,128)(2,1)S(1)}, bf16[16,4096]{1,0:T(8,128)(2,1)S(1)}, bf16[16,4096]{1,0:T(8,128)(2,1)S(1)}, s32[4,64]{1,0:T(4,128)S(1)}) custom-call(s32[1]{0:T(128)} %bitcast.half_ref, s32[2,64]{1,0:T(2,128)} %bitcast.34, s32[2,64]{1,0:T(2,128)} %bitcast.35, s32[2,64]{1,0:T(2,128)} %bitcast.36, ...), custom_call_target="tpu_custom_call" | custom-call | flops 68719476736 | bytes 1572864 | tf_op jit(solution)/shard_map/pallas_call | solution.py:92
  2.5 2.3 %collective-permute-start.3 = (bf16[16,4096]{1,0:T(8,128)(2,1)S(1)}, bf16[16,4096]{1,0:T(8,128)(2,1)S(1)}, u32[]{:S(2)}, u32[]{:S(2)}) collective-permute-start(bf16[16,4096]{1,0:T(8,128)(2,1)S(1)} %get-tuple-element.20.refs_0_), channel_id=1, source_target_pairs={{0,3},{1,2},{2,1},{3,0},{4,7},{5,6},{6,5},{7,4},{8,11},{9,10},{10,... | collective-permute-start | bytes 393224 | tf_op jit(solution)/shard_map/ppermute | solution.py:302
  4.8 0.2 collective-permute-start.2
  4.9 0.2 collective-permute-start.1
  5.2 2.3 %collective-permute-start.4 = (bf16[16,4096]{1,0:T(8,128)(2,1)S(1)}, bf16[16,4096]{1,0:T(8,128)(2,1)S(1)}, u32[]{:S(2)}, u32[]{:S(2)}) collective-permute-start(bf16[16,4096]{1,0:T(8,128)(2,1)S(1)} %get-tuple-element.21), channel_id=1, source_target_pairs={{0,4},{1,5},{2,6},{3,7},{4,0},{5,1},{6,2},{7,3},{8,12},{9,13},{10,... | collective-permute-start | bytes 393224 | tf_op jit(solution)/shard_map/ppermute | solution.py:302
  7.5 0.1 collective-permute-start.13
  7.5 5.0 %collective-permute-done.4.refs_4_ = bf16[16,4096]{1,0:T(8,128)(2,1)S(1)} collective-permute-done((bf16[16,4096]{1,0:T(8,128)(2,1)S(1)}, bf16[16,4096]{1,0:T(8,128)(2,1)S(1)}, u32[]{:S(2)}, u32[]{:S(2)}) %collective-permute-start.4) | collective-permute-done | bytes 131104 | tf_op jit(solution)/shard_map/ppermute | solution.py:302
  12.6 3.2 %collective-permute-start.7 = (bf16[16,4096]{1,0:T(8,128)(2,1)S(1)}, bf16[16,4096]{1,0:T(8,128)(2,1)S(1)}, u32[]{:S(2)}, u32[]{:S(2)}) collective-permute-start(bf16[16,4096]{1,0:T(8,128)(2,1)S(1)} %collective-permute-done.4.refs_4_), channel_id=1, source_target_pairs={{0,3},{1,2},{2,1},{3,0},{4,7},{5,6},{6,5},{7,4},{8,11},{9,10},{10,... | collective-permute-start | bytes 393224 | tf_op jit(solution)/shard_map/ppermute | solution.py:302
  15.7 2.8 %collective-permute-done.13 = bf16[16,4096]{1,0:T(8,128)(2,1)S(1)} collective-permute-done((bf16[16,4096]{1,0:T(8,128)(2,1)S(1)}, bf16[16,4096]{1,0:T(8,128)(2,1)S(1)}, u32[]{:S(2)}, u32[]{:S(2)}) %collective-permute-start.13) | collective-permute-done | bytes 131104 | tf_op jit(solution)/shard_map/ppermute | solution.py:302
  18.5 0.2 collective-permute-start.6
  18.6 0.0 collective-permute-done.3.refs_3_
  18.6 2.1 %collective-permute-start.5 = (bf16[16,4096]{1,0:T(8,128)(2,1)S(1)}, bf16[16,4096]{1,0:T(8,128)(2,1)S(1)}, u32[]{:S(2)}, u32[]{:S(2)}) collective-permute-start(bf16[16,4096]{1,0:T(8,128)(2,1)S(1)} %collective-permute-done.4.refs_4_), channel_id=1, source_target_pairs={{0,1},{1,0},{2,3},{3,2},{4,5},{5,4},{6,7},{7,6},{8,9},{9,8},{10,11... | collective-permute-start | bytes 393224 | tf_op jit(solution)/shard_map/ppermute | solution.py:302
  20.8 0.0 collective-permute-done.2.refs_2_
  20.8 1.2 %collective-permute-start.16 = (bf16[32,4096]{1,0:T(8,128)(2,1)S(1)}, bf16[32,4096]{1,0:T(8,128)(2,1)S(1)}, u32[]{:S(2)}, u32[]{:S(2)}) collective-permute-start(bf16[32,4096]{1,0:T(8,128)(2,1)S(1)} %constant_dynamic-update-slice_fusion.refs_0_), channel_id=1, source_target_pairs={{0,3},{1,2},{2,1},{3,0},{4,7},{5,6},{6,5},{7,4},{8,11},{9,10},{10,... | collective-permute-start | bytes 786440 | tf_op jit(solution)/shard_map/ppermute | solution.py:302
  22.0 0.0 collective-permute-done.1.refs_1_
  22.0 0.4 collective-permute-start.15
  22.4 0.0 collective-permute-done.7.refs_7_
  22.4 1.2 %collective-permute-start.14 = (bf16[32,4096]{1,0:T(8,128)(2,1)S(1)}, bf16[32,4096]{1,0:T(8,128)(2,1)S(1)}, u32[]{:S(2)}, u32[]{:S(2)}) collective-permute-start(bf16[32,4096]{1,0:T(8,128)(2,1)S(1)} %constant_dynamic-update-slice_fusion.refs_0_), channel_id=1, source_target_pairs={{0,1},{1,0},{2,3},{3,2},{4,5},{5,4},{6,7},{7,6},{8,9},{9,8},{10,11... | collective-permute-start | bytes 786440 | tf_op jit(solution)/shard_map/ppermute | solution.py:302
  23.6 0.0 collective-permute-done.6.refs_6_
  23.6 2.0 %collective-permute-done.5.refs_5_ = bf16[16,4096]{1,0:T(8,128)(2,1)S(1)} collective-permute-done((bf16[16,4096]{1,0:T(8,128)(2,1)S(1)}, bf16[16,4096]{1,0:T(8,128)(2,1)S(1)}, u32[]{:S(2)}, u32[]{:S(2)}) %collective-permute-start.5) | collective-permute-done | bytes 131104 | tf_op jit(solution)/shard_map/ppermute | solution.py:302
  25.5 0.0 copy-done
  25.5 7.7 %shard_map.130 = (bf16[128,4096]{1,0:T(8,128)(2,1)S(1)}, bf16[128,1792]{1,0:T(8,128)(2,1)S(1)}, bf16[128,1792]{1,0:T(8,128)(2,1)S(1)}, bf16[128,1792]{1,0:T(8,128)(2,1)S(1)}) custom-call(s32[1]{0:T(128)} %bitcast.9.index_ref, bf16[16,4096]{1,0:T(8,128)(2,1)S(1)} %get-tuple-element.20.refs_0_, bf16[16,4096]{1,0:T(8,128)(2,1)S(1)} %collective-permute-done.1.refs_1_, ...), custom_call_target="tpu_custom_call" | custom-call | flops 1879048192 | bytes 14680064 | tf_op jit(solution)/shard_map/pallas_call | solution.py:135
  33.2 0.0 slice-done
  33.2 0.0 slice-done.1
  33.3 0.0 slice-done.2
  33.3 0.0 slice-done.3
  33.3 0.0 copy-start.1
  33.3 5.2 %copy-done.1 = bf16[1,4096,1792]{2,1,0:T(8,128)(2,1)S(1)} copy-done((bf16[1,4096,1792]{2,1,0:T(8,128)(2,1)S(1)}, bf16[1,4096,1792]{2,1,0:T(8,128)(2,1)}, u32[]{:S(2)}) %copy-start.1) | copy-done | bytes 14680088
  38.5 9.4 %shard_map.131 = (bf16[32,4096]{1,0:T(8,128)(2,1)S(1)}, bf16[32,4096]{1,0:T(8,128)(2,1)S(1)}, bf16[32,4096]{1,0:T(8,128)(2,1)S(1)}, bf16[32,4096]{1,0:T(8,128)(2,1)S(1)}) custom-call(s32[1]{0:T(128)} %bitcast.9.index_ref, bf16[128,1792]{1,0:T(8,128)(2,1)S(1)} %get-tuple-element.22.refs_0_.refs_4_, bf16[128,1792]{1,0:T(8,128)(2,1)S(1)} %get-tuple-element.23.refs_1_.right, ...), custom_call_target="tpu_custom_call" | custom-call | flops 3758096384 | bytes 29360128 | tf_op jit(solution)/shard_map/pallas_call | solution.py:174
  47.9 2.8 %collective-permute-start.8 = (bf16[32,4096]{1,0:T(8,128)(2,1)S(1)}, bf16[32,4096]{1,0:T(8,128)(2,1)S(1)}, u32[]{:S(2)}, u32[]{:S(2)}) collective-permute-start(bf16[32,4096]{1,0:T(8,128)(2,1)S(1)} %get-tuple-element.25), channel_id=1, source_target_pairs={{0,1},{1,0},{2,3},{3,2},{4,5},{5,4},{6,7},{7,6},{8,9},{9,8},{10,11... | collective-permute-start | bytes 786440 | tf_op jit(solution)/shard_map/ppermute | solution.py:302
  50.7 5.3 %collective-permute-start.9 = (bf16[32,4096]{1,0:T(8,128)(2,1)S(1)}, bf16[32,4096]{1,0:T(8,128)(2,1)S(1)}, u32[]{:S(2)}, u32[]{:S(2)}) collective-permute-start(bf16[32,4096]{1,0:T(8,128)(2,1)S(1)} %get-tuple-element.26), channel_id=1, source_target_pairs={{0,2},{1,3},{2,0},{3,1},{4,6},{5,7},{6,4},{7,5},{8,10},{9,11},{10,... | collective-permute-start | bytes 786440 | tf_op jit(solution)/shard_map/ppermute | solution.py:302
  56.0 0.0 collective-permute-done.16.refs_3_
  56.0 0.0 collective-permute-start.10
  56.0 6.6 %shard_map.135 = bf16[1792,4096]{1,0:T(8,128)(2,1)} custom-call(bf16[128,1792]{1,0:T(8,128)(2,1)S(1)} %get-tuple-element.32.left, bf16[128,4096]{1,0:T(8,128)(2,1)S(1)} %get-tuple-element.33.right), custom_call_target="tpu_custom_call" | custom-call | flops 1879048192 | bytes 14680064 | tf_op jit(solution)/shard_map/pallas_call | solution.py:246
  62.6 0.0 collective-permute-done.15.refs_2_
  62.6 5.0 %collective-permute-start = (s32[4,64]{1,0:T(4,128)S(1)}, s32[4,64]{1,0:T(4,128)S(1)}, u32[]{:S(2)}, u32[]{:S(2)}) collective-permute-start(s32[4,64]{1,0:T(4,128)S(1)} %get-tuple-element.19), channel_id=1, source_target_pairs={{8,0},{9,1},{10,2},{11,3},{12,4},{13,5},{14,6},{15,7},{16,8},{17,9... | collective-permute-start | bytes 3080 | tf_op jit(solution)/shard_map/ppermute | solution.py:310
  67.7 0.0 collective-permute-done.14.refs_1_
  67.7 8.5 %shard_map.133 = (bf16[4096,1792]{1,0:T(8,128)(2,1)}, bf16[128,4096]{1,0:T(8,128)(2,1)S(1)}) custom-call(s32[1]{0:T(128)} %bitcast.9.index_ref, bf16[32,4096]{1,0:T(8,128)(2,1)S(1)} %constant_dynamic-update-slice_fusion.refs_0_, bf16[32,4096]{1,0:T(8,128)(2,1)S(1)} %collective-permute-done.14.refs_1_, bf16[32,4096]{1,0:T(8,128)(2,1)S(1)} %collective-permute-done.15.refs_2_, ...), custom_call_target="tpu_custom_call" | custom-call | flops 1879048192 | bytes 14680064 | tf_op jit(solution)/shard_map/pallas_call | solution.py:263
  76.2 0.0 collective-permute-done.8
  76.2 0.0 collective-permute-done.9
  76.2 0.0 collective-permute-done.10
  76.2 0.1 add_convert_fusion
  76.4 4.9 %collective-permute-start.12 = (bf16[16,4096]{1,0:T(8,128)(2,1)S(1)}, bf16[16,4096]{1,0:T(8,128)(2,1)S(1)}, u32[]{:S(2)}, u32[]{:S(2)}) collective-permute-start(bf16[16,4096]{1,0:T(8,128)(2,1)S(1)} %get-tuple-element.34), channel_id=1, source_target_pairs={{8,4},{9,5},{10,6},{11,7},{12,0},{13,1},{14,2},{15,3},{16,12},{17,... | collective-permute-start | bytes 393224 | tf_op jit(solution)/shard_map/ppermute | solution.py:310
  81.3 2.4 %collective-permute-start.11 = (bf16[16,4096]{1,0:T(8,128)(2,1)S(1)}, bf16[16,4096]{1,0:T(8,128)(2,1)S(1)}, u32[]{:S(2)}, u32[]{:S(2)}) collective-permute-start(bf16[16,4096]{1,0:T(8,128)(2,1)S(1)} %get-tuple-element.35), channel_id=1, source_target_pairs={{8,0},{9,1},{10,2},{11,3},{12,4},{13,5},{14,6},{15,7},{16,8},{17,9... | collective-permute-start | bytes 393224 | tf_op jit(solution)/shard_map/ppermute | solution.py:310
  83.6 7.0 %shard_map.134 = bf16[4096,1792]{1,0:T(8,128)(2,1)} custom-call(bf16[128,4096]{1,0:T(8,128)(2,1)S(1)} %get-tuple-element.31.left, bf16[128,1792]{1,0:T(8,128)(2,1)S(1)} %get-tuple-element.23.refs_1_.right), custom_call_target="tpu_custom_call" | custom-call | flops 1879048192 | bytes 14680064 | tf_op jit(solution)/shard_map/pallas_call | solution.py:246
  90.7 0.0 collective-permute-done.tables
  90.7 0.0 collective-permute-done.12.refs_1_
  90.7 0.0 collective-permute-done.11.refs_0_
  90.7 1.3 %shard_map.132 = bf16[64,4096]{1,0:T(8,128)(2,1)} custom-call(s32[1]{0:T(128)} %bitcast.half_ref, s32[4,64]{1,0:T(4,128)S(1)} %collective-permute-done.tables, bf16[16,4096]{1,0:T(8,128)(2,1)S(1)} %collective-permute-done.11.refs_0_, bf16[16,4096]{1,0:T(8,128)(2,1)S(1)} %collective-permute-done.12.refs_1_), custom_call_target="tpu_custom_call" | custom-call | tf_op jit(solution)/shard_map/pallas_call | solution.py:291
  (4 shorter events, 0.0 us)
Async XLA Ops:
  0.6 32.6 %slice-start = ((s8[14680064]{0:T(1024)(128)(4,1)}), s8[4194304]{0:T(1024)(128)(4,1)S(1)}, s32[]{:S(2)}) async-start(s8[14680064]{0:T(1024)(128)(4,1)} %bitcast.23), calls=%async_computation | async-start | bytes 8388608
  0.7 24.9 %copy-start = (bf16[1,1792,4096]{2,1,0:T(8,128)(2,1)S(1)}, bf16[1,1792,4096]{2,1,0:T(8,128)(2,1)}, u32[]{:S(2)}) copy-start(bf16[1,1792,4096]{2,1,0:T(8,128)(2,1)} %param.19) | copy-start | bytes 44040196
  0.7 32.6 %slice-start.1 = ((s8[14680064]{0:T(1024)(128)(4,1)}), s8[4194304]{0:T(1024)(128)(4,1)S(1)}, s32[]{:S(2)}) async-start(s8[14680064]{0:T(1024)(128)(4,1)} %bitcast.23), calls=%async_computation.1 | async-start | bytes 8388608
  0.7 32.6 %slice-start.2 = ((s8[14680064]{0:T(1024)(128)(4,1)}), s8[4194304]{0:T(1024)(128)(4,1)S(1)}, s32[]{:S(2)}) async-start(s8[14680064]{0:T(1024)(128)(4,1)} %bitcast.23), calls=%async_computation.2 | async-start | bytes 8388608
  0.7 32.6 %slice-start.3 = ((s8[14680064]{0:T(1024)(128)(4,1)}), s8[2097152]{0:T(1024)(128)(4,1)S(1)}, s32[]{:S(2)}) async-start(s8[14680064]{0:T(1024)(128)(4,1)} %bitcast.23), calls=%async_computation.3 | async-start | bytes 4194304
  2.5 16.2 %collective-permute-start.3 = (bf16[16,4096]{1,0:T(8,128)(2,1)S(1)}, bf16[16,4096]{1,0:T(8,128)(2,1)S(1)}, u32[]{:S(2)}, u32[]{:S(2)}) collective-permute-start(bf16[16,4096]{1,0:T(8,128)(2,1)S(1)} %get-tuple-element.20.refs_0_), channel_id=1, source_target_pairs={{0,3},{1,2},{2,1},{3,0},{4,7},{5,6},{6,5},{7,4},{8,11},{9,10},{10,... | collective-permute-start | bytes 393224 | tf_op jit(solution)/shard_map/ppermute | solution.py:302
  4.8 16.0 %collective-permute-start.2 = (bf16[16,4096]{1,0:T(8,128)(2,1)S(1)}, bf16[16,4096]{1,0:T(8,128)(2,1)S(1)}, u32[]{:S(2)}, u32[]{:S(2)}) collective-permute-start(bf16[16,4096]{1,0:T(8,128)(2,1)S(1)} %get-tuple-element.20.refs_0_), channel_id=1, source_target_pairs={{0,2},{1,3},{2,0},{3,1},{4,6},{5,7},{6,4},{7,5},{8,10},{9,11},{10,... | collective-permute-start | bytes 393224 | tf_op jit(solution)/shard_map/ppermute | solution.py:302
  4.9 17.1 %collective-permute-start.1 = (bf16[16,4096]{1,0:T(8,128)(2,1)S(1)}, bf16[16,4096]{1,0:T(8,128)(2,1)S(1)}, u32[]{:S(2)}, u32[]{:S(2)}) collective-permute-start(bf16[16,4096]{1,0:T(8,128)(2,1)S(1)} %get-tuple-element.20.refs_0_), channel_id=1, source_target_pairs={{0,1},{1,0},{2,3},{3,2},{4,5},{5,4},{6,7},{7,6},{8,9},{9,8},{10,11... | collective-permute-start | bytes 393224 | tf_op jit(solution)/shard_map/ppermute | solution.py:302
  5.2 7.4 %collective-permute-start.4 = (bf16[16,4096]{1,0:T(8,128)(2,1)S(1)}, bf16[16,4096]{1,0:T(8,128)(2,1)S(1)}, u32[]{:S(2)}, u32[]{:S(2)}) collective-permute-start(bf16[16,4096]{1,0:T(8,128)(2,1)S(1)} %get-tuple-element.21), channel_id=1, source_target_pairs={{0,4},{1,5},{2,6},{3,7},{4,0},{5,1},{6,2},{7,3},{8,12},{9,13},{10,... | collective-permute-start | bytes 393224 | tf_op jit(solution)/shard_map/ppermute | solution.py:302
  7.5 11.0 %collective-permute-start.13 = (bf16[16,4096]{1,0:T(8,128)(2,1)S(1)}, bf16[16,4096]{1,0:T(8,128)(2,1)S(1)}, u32[]{:S(2)}, u32[]{:S(2)}) collective-permute-start(bf16[16,4096]{1,0:T(8,128)(2,1)S(1)} %get-tuple-element.29), channel_id=1, source_target_pairs={{0,4},{1,5},{2,6},{3,7},{4,0},{5,1},{6,2},{7,3},{8,12},{9,13},{10,... | collective-permute-start | bytes 393224 | tf_op jit(solution)/shard_map/ppermute | solution.py:302
  12.6 9.8 %collective-permute-start.7 = (bf16[16,4096]{1,0:T(8,128)(2,1)S(1)}, bf16[16,4096]{1,0:T(8,128)(2,1)S(1)}, u32[]{:S(2)}, u32[]{:S(2)}) collective-permute-start(bf16[16,4096]{1,0:T(8,128)(2,1)S(1)} %collective-permute-done.4.refs_4_), channel_id=1, source_target_pairs={{0,3},{1,2},{2,1},{3,0},{4,7},{5,6},{6,5},{7,4},{8,11},{9,10},{10,... | collective-permute-start | bytes 393224 | tf_op jit(solution)/shard_map/ppermute | solution.py:302
  18.5 5.1 %collective-permute-start.6 = (bf16[16,4096]{1,0:T(8,128)(2,1)S(1)}, bf16[16,4096]{1,0:T(8,128)(2,1)S(1)}, u32[]{:S(2)}, u32[]{:S(2)}) collective-permute-start(bf16[16,4096]{1,0:T(8,128)(2,1)S(1)} %collective-permute-done.4.refs_4_), channel_id=1, source_target_pairs={{0,2},{1,3},{2,0},{3,1},{4,6},{5,7},{6,4},{7,5},{8,10},{9,11},{10,... | collective-permute-start | bytes 393224 | tf_op jit(solution)/shard_map/ppermute | solution.py:302
  18.6 6.9 %collective-permute-start.5 = (bf16[16,4096]{1,0:T(8,128)(2,1)S(1)}, bf16[16,4096]{1,0:T(8,128)(2,1)S(1)}, u32[]{:S(2)}, u32[]{:S(2)}) collective-permute-start(bf16[16,4096]{1,0:T(8,128)(2,1)S(1)} %collective-permute-done.4.refs_4_), channel_id=1, source_target_pairs={{0,1},{1,0},{2,3},{3,2},{4,5},{5,4},{6,7},{7,6},{8,9},{9,8},{10,11... | collective-permute-start | bytes 393224 | tf_op jit(solution)/shard_map/ppermute | solution.py:302
  20.8 35.2 %collective-permute-start.16 = (bf16[32,4096]{1,0:T(8,128)(2,1)S(1)}, bf16[32,4096]{1,0:T(8,128)(2,1)S(1)}, u32[]{:S(2)}, u32[]{:S(2)}) collective-permute-start(bf16[32,4096]{1,0:T(8,128)(2,1)S(1)} %constant_dynamic-update-slice_fusion.refs_0_), channel_id=1, source_target_pairs={{0,3},{1,2},{2,1},{3,0},{4,7},{5,6},{6,5},{7,4},{8,11},{9,10},{10,... | collective-permute-start | bytes 786440 | tf_op jit(solution)/shard_map/ppermute | solution.py:302
  22.0 40.6 %collective-permute-start.15 = (bf16[32,4096]{1,0:T(8,128)(2,1)S(1)}, bf16[32,4096]{1,0:T(8,128)(2,1)S(1)}, u32[]{:S(2)}, u32[]{:S(2)}) collective-permute-start(bf16[32,4096]{1,0:T(8,128)(2,1)S(1)} %constant_dynamic-update-slice_fusion.refs_0_), channel_id=1, source_target_pairs={{0,2},{1,3},{2,0},{3,1},{4,6},{5,7},{6,4},{7,5},{8,10},{9,11},{10,... | collective-permute-start | bytes 786440 | tf_op jit(solution)/shard_map/ppermute | solution.py:302
  22.4 45.3 %collective-permute-start.14 = (bf16[32,4096]{1,0:T(8,128)(2,1)S(1)}, bf16[32,4096]{1,0:T(8,128)(2,1)S(1)}, u32[]{:S(2)}, u32[]{:S(2)}) collective-permute-start(bf16[32,4096]{1,0:T(8,128)(2,1)S(1)} %constant_dynamic-update-slice_fusion.refs_0_), channel_id=1, source_target_pairs={{0,1},{1,0},{2,3},{3,2},{4,5},{5,4},{6,7},{7,6},{8,9},{9,8},{10,11... | collective-permute-start | bytes 786440 | tf_op jit(solution)/shard_map/ppermute | solution.py:302
  33.3 5.2 %copy-start.1 = (bf16[1,4096,1792]{2,1,0:T(8,128)(2,1)S(1)}, bf16[1,4096,1792]{2,1,0:T(8,128)(2,1)}, u32[]{:S(2)}) copy-start(bf16[1,4096,1792]{2,1,0:T(8,128)(2,1)} %param.18) | copy-start | bytes 44040196
  47.9 28.3 %collective-permute-start.8 = (bf16[32,4096]{1,0:T(8,128)(2,1)S(1)}, bf16[32,4096]{1,0:T(8,128)(2,1)S(1)}, u32[]{:S(2)}, u32[]{:S(2)}) collective-permute-start(bf16[32,4096]{1,0:T(8,128)(2,1)S(1)} %get-tuple-element.25), channel_id=1, source_target_pairs={{0,1},{1,0},{2,3},{3,2},{4,5},{5,4},{6,7},{7,6},{8,9},{9,8},{10,11... | collective-permute-start | bytes 786440 | tf_op jit(solution)/shard_map/ppermute | solution.py:302
  50.7 25.5 %collective-permute-start.9 = (bf16[32,4096]{1,0:T(8,128)(2,1)S(1)}, bf16[32,4096]{1,0:T(8,128)(2,1)S(1)}, u32[]{:S(2)}, u32[]{:S(2)}) collective-permute-start(bf16[32,4096]{1,0:T(8,128)(2,1)S(1)} %get-tuple-element.26), channel_id=1, source_target_pairs={{0,2},{1,3},{2,0},{3,1},{4,6},{5,7},{6,4},{7,5},{8,10},{9,11},{10,... | collective-permute-start | bytes 786440 | tf_op jit(solution)/shard_map/ppermute | solution.py:302
  56.0 20.2 %collective-permute-start.10 = (bf16[32,4096]{1,0:T(8,128)(2,1)S(1)}, bf16[32,4096]{1,0:T(8,128)(2,1)S(1)}, u32[]{:S(2)}, u32[]{:S(2)}) collective-permute-start(bf16[32,4096]{1,0:T(8,128)(2,1)S(1)} %get-tuple-element.27), channel_id=1, source_target_pairs={{0,3},{1,2},{2,1},{3,0},{4,7},{5,6},{6,5},{7,4},{8,11},{9,10},{10,... | collective-permute-start | bytes 786440 | tf_op jit(solution)/shard_map/ppermute | solution.py:302
  62.6 28.1 %collective-permute-start = (s32[4,64]{1,0:T(4,128)S(1)}, s32[4,64]{1,0:T(4,128)S(1)}, u32[]{:S(2)}, u32[]{:S(2)}) collective-permute-start(s32[4,64]{1,0:T(4,128)S(1)} %get-tuple-element.19), channel_id=1, source_target_pairs={{8,0},{9,1},{10,2},{11,3},{12,4},{13,5},{14,6},{15,7},{16,8},{17,9... | collective-permute-start | bytes 3080 | tf_op jit(solution)/shard_map/ppermute | solution.py:310
  76.4 14.3 %collective-permute-start.12 = (bf16[16,4096]{1,0:T(8,128)(2,1)S(1)}, bf16[16,4096]{1,0:T(8,128)(2,1)S(1)}, u32[]{:S(2)}, u32[]{:S(2)}) collective-permute-start(bf16[16,4096]{1,0:T(8,128)(2,1)S(1)} %get-tuple-element.34), channel_id=1, source_target_pairs={{8,4},{9,5},{10,6},{11,7},{12,0},{13,1},{14,2},{15,3},{16,12},{17,... | collective-permute-start | bytes 393224 | tf_op jit(solution)/shard_map/ppermute | solution.py:310
  81.3 9.4 %collective-permute-start.11 = (bf16[16,4096]{1,0:T(8,128)(2,1)S(1)}, bf16[16,4096]{1,0:T(8,128)(2,1)S(1)}, u32[]{:S(2)}, u32[]{:S(2)}) collective-permute-start(bf16[16,4096]{1,0:T(8,128)(2,1)S(1)} %get-tuple-element.35), channel_id=1, source_target_pairs={{8,0},{9,1},{10,2},{11,3},{12,4},{13,5},{14,6},{15,7},{16,8},{17,9... | collective-permute-start | bytes 393224 | tf_op jit(solution)/shard_map/ppermute | solution.py:310
